TPU v7x, 32 devices: a whole 2x2x4 slice. The times are simulated.
32 devices in a mesh: ctx: 8 (over y, x, core), shard: 4 (over z).
Axes of the slice: x: 2, y: 2, z: 4, core: 2. Of those that a mesh axis runs over, the one named last changes fastest.
Arguments:
- hidden_in: bfloat16 [8, 1024, 768], P('shard', 'ctx'), may hold values from -6 to 6
- block_of: int32 [16], replicated, may hold values from 0 to 15, each once
- lengths: int32 [8], replicated, may hold values from 256 to 1024, as said below
- attn_latent: float32 [4, 768, 768], P(None, 'shard'), may hold values from -1.25 to 1.25
- ffn_in_latent: float32 [768, 3072], P('shard'), may hold values from -1.25 to 1.25
- ffn_out_latent: float32 [3072, 768], P('shard'), may hold values from -1.25 to 1.25
- student_vec: float32 [12, 768], replicated
- teacher_attn: bfloat16 [4, 768, 768], P(None, 'shard'), may hold values from -0.3125 to 0.3125
- teacher_ffn_in: bfloat16 [768, 3072], P('shard'), may hold values from -0.21875 to 0.21875
- teacher_ffn_out: bfloat16 [3072, 768], P('shard'), may hold values from -0.109375 to 0.109375
- teacher_vec: float32 [12, 768], replicated
Outputs:
- output: bfloat16 [8, 1024, 768], P('shard', 'ctx')
- statistics: float32 [4], replicated
- grad_hidden: float32 [8, 1024, 768], P('shard', 'ctx')
- grad_attn_latent: float32 [4, 768, 768], P(None, 'shard')
- grad_ffn_in_latent: float32 [768, 3072], P('shard')
- grad_ffn_out_latent: float32 [3072, 768], P('shard')
- grad_student_vec: float32 [11, 768], replicated
- grad_query_bias: float32 [768], replicated
Inputs may be any that keep to these rules, and one draw needn't show every extreme that they name: `block_of`: every block of 64 places of a sequence is named once; entry q holds the block that lies at layout places q * 64 to (q + 1) * 64 - 1, the same for every sequence. `lengths`: A token is valid where its place is below its sequence's length; some sequence has length 1024.
All inputs are finite; a program needn't handle non-finite values.
Results may differ from a plain program's by a relative error of at most 0.0097.
Values may be sent and summed in bfloat16 or wider, within the bound.
No kernel may reach another device: no remote copies, remote signals or barrier semaphores. Data moves between devices by JAX's collectives and lax.ppermute only.
A program may use at most 320 MiB of HBM per device.

v0:
```python
import jax
import jax.numpy as jnp
from jax import lax
from jax.sharding import PartitionSpec as P

D = 768
HEADS = 12
HEAD_DIM = 64
FF = 3072
BLK = 64
norm_eps = 1e-05
attn_gains = (2.0, 2.0, 1.0, 4.0)
heads_block = 4
masked_score = -1e30


def layer_norm(values, gain, shift):
    middle = jnp.mean(values, axis=-1, keepdims=True)
    centred = values - middle
    spread = jnp.mean(centred * centred, axis=-1, keepdims=True)
    return centred * lax.rsqrt(spread + norm_eps) * gain + shift


def gelu_exact(values):
    return jax.nn.gelu(values, approximate=False)


def matmul(left_side, right_side):
    return jnp.dot(left_side, right_side, preferred_element_type=jnp.float32)


def left_product(left_side, right_side):
    return lax.dot_general(
        left_side, right_side, (((0,), (0,)), ((), ())), preferred_element_type=jnp.float32
    )


def right_product(left_side, right_side):
    return lax.dot_general(
        left_side, right_side, (((1,), (1,)), ((), ())), preferred_element_type=jnp.float32
    )


def binarize(latent, column_sum, gain, fan_in):
    return (gain * (column_sum / fan_in) * jnp.sign(latent) * fan_in ** (-0.5)).astype(jnp.bfloat16)


def positions_of(block_of):
    return (block_of[:, None] * BLK + jnp.arange(BLK, dtype=jnp.int32)[None, :]).reshape(
        block_of.shape[0] * BLK
    )


def split_heads(row_matrix, head_group):
    begin = head_group * heads_block * HEAD_DIM
    piece = row_matrix[:, begin : begin + heads_block * HEAD_DIM]
    return piece.reshape(row_matrix.shape[0], heads_block, HEAD_DIM)


def join_heads(parts_list):
    return jnp.concatenate(
        [part_one.reshape(part_one.shape[0], heads_block * HEAD_DIM) for part_one in parts_list],
        axis=1,
    )


def attend_forward(query_rows, key_all, value_all, query_pos, key_pos):
    score_scale = HEAD_DIM ** (-0.5)
    allowed = (query_pos[:, None] >= key_pos[None, :])[None]
    head_outs = []
    log_sums = []
    for head_group in range(HEADS // heads_block):
        q_heads = split_heads(query_rows, head_group)
        k_heads = split_heads(key_all, head_group)
        v_heads = split_heads(value_all, head_group)
        scores = (
            jnp.einsum("qhd,khd->hqk", q_heads, k_heads, preferred_element_type=jnp.float32)
            * score_scale
        )
        scores = jnp.where(allowed, scores, masked_score)
        row_peak = jnp.max(scores, axis=-1, keepdims=True)
        row_total = jnp.sum(jnp.exp(scores - row_peak), axis=-1, keepdims=True)
        log_total = row_peak + jnp.log(row_total)
        prob_rows = jnp.exp(scores - log_total).astype(jnp.bfloat16)
        head_outs.append(
            jnp.einsum("hqk,khd->qhd", prob_rows, v_heads, preferred_element_type=jnp.float32)
        )
        log_sums.append(log_total[..., 0])
    return (join_heads(head_outs), jnp.concatenate(log_sums, axis=0))


def attend_query_back(query_rows, key_all, value_all, grad_rows, log_sums, query_pos, key_pos):
    score_scale = HEAD_DIM ** (-0.5)
    allowed = (query_pos[:, None] >= key_pos[None, :])[None]
    grad_q_parts = []
    delta_parts = []
    grad_k_parts = []
    grad_v_parts = []
    for head_group in range(HEADS // heads_block):
        head_span = slice(head_group * heads_block, (head_group + 1) * heads_block)
        q_heads = split_heads(query_rows, head_group)
        k_heads = split_heads(key_all, head_group)
        v_heads = split_heads(value_all, head_group)
        g_heads = split_heads(grad_rows, head_group)
        scores = (
            jnp.einsum("qhd,khd->hqk", q_heads, k_heads, preferred_element_type=jnp.float32)
            * score_scale
        )
        scores = jnp.where(allowed, scores, masked_score)
        prob_rows = jnp.exp(scores - log_sums[head_span][:, :, None])
        grad_prob = jnp.einsum("qhd,khd->hqk", g_heads, v_heads, preferred_element_type=jnp.float32)
        row_delta = jnp.sum(prob_rows * grad_prob, axis=-1)
        grad_score = (prob_rows * (grad_prob - row_delta[:, :, None])).astype(jnp.bfloat16)
        grad_q_parts.append(
            jnp.einsum("hqk,khd->qhd", grad_score, k_heads, preferred_element_type=jnp.float32)
            * score_scale
        )
        delta_parts.append(row_delta)
        grad_k_parts.append(
            jnp.einsum("hqk,qhd->khd", grad_score, q_heads, preferred_element_type=jnp.float32)
            * score_scale
        )
        grad_v_parts.append(
            jnp.einsum(
                "hqk,qhd->khd",
                prob_rows.astype(jnp.bfloat16),
                g_heads,
                preferred_element_type=jnp.float32,
            )
        )
    return (
        join_heads(grad_q_parts),
        jnp.concatenate(delta_parts, axis=0),
        join_heads(grad_k_parts),
        join_heads(grad_v_parts),
    )


def project(flat_bf, w_attn, vector, seq_here):
    query_rows = (matmul(flat_bf, w_attn[0]) + vector[0]).astype(jnp.bfloat16)
    key_rows = matmul(flat_bf, w_attn[1]).astype(jnp.bfloat16)
    value_rows = (matmul(flat_bf, w_attn[2]) + vector[1]).astype(jnp.bfloat16)
    return (
        query_rows.reshape(seq_here, -1, D),
        key_rows.reshape(seq_here, -1, D),
        value_rows.reshape(seq_here, -1, D),
    )


def dense_part(flat_rows, heads_bf, w_out, w_in, w_down, vector):
    branch = matmul(heads_bf, w_out) + vector[2]
    first_norm = layer_norm(flat_rows + branch, vector[4], vector[5])
    first_bf = first_norm.astype(jnp.bfloat16)
    inner_pre = matmul(first_bf, w_in) + vector[8:].reshape(-1)
    activated = gelu_exact(inner_pre).astype(jnp.bfloat16)
    feed_out = matmul(activated, w_down) + vector[3]
    second_sum = first_norm + feed_out
    output = layer_norm(second_sum, vector[6], vector[7])
    return (branch, first_norm, first_bf, inner_pre, activated, feed_out, second_sum, output)


def body(
    hidden_in,
    block_of,
    lengths,
    attn_latent,
    ffn_in_latent,
    ffn_out_latent,
    student_vec,
    teacher_attn,
    teacher_ffn_in,
    teacher_ffn_out,
    teacher_vec,
):
    seq_here, rows_here = (hidden_in.shape[0], hidden_in.shape[1])
    token_count = seq_here * rows_here
    ctx_index = lax.axis_index("ctx")
    shard_index = lax.axis_index("shard")
    key_pos = positions_of(block_of)
    query_pos = lax.dynamic_slice_in_dim(key_pos, ctx_index * rows_here, rows_here)
    own_lengths = lax.dynamic_slice_in_dim(lengths, shard_index * seq_here, seq_here)
    valid_rows = (
        (query_pos[None, :] < own_lengths[:, None]).astype(jnp.float32).reshape(token_count, 1)
    )
    valid_count = jnp.sum(lengths.astype(jnp.float32))
    loss_scale = valid_count * D
    attn_gain = jnp.asarray(attn_gains, dtype=jnp.float32)[:, None, None]
    full_attn, full_in, full_out = (
        lax.all_gather(attn_latent, "shard", axis=1, tiled=True),
        lax.all_gather(ffn_in_latent, "shard", axis=0, tiled=True),
        lax.all_gather(ffn_out_latent, "shard", axis=0, tiled=True),
    )
    bin_attn = binarize(full_attn, jnp.sum(jnp.abs(full_attn), axis=1, keepdims=True), attn_gain, D)
    bin_in = binarize(full_in, jnp.sum(jnp.abs(full_in), axis=0, keepdims=True), 1.0, D)
    bin_out = binarize(full_out, jnp.sum(jnp.abs(full_out), axis=0, keepdims=True), 1.0, FF)
    teach_attn, teach_in, teach_out = (
        lax.all_gather(teacher_attn, "shard", axis=1, tiled=True),
        lax.all_gather(teacher_ffn_in, "shard", axis=0, tiled=True),
        lax.all_gather(teacher_ffn_out, "shard", axis=0, tiled=True),
    )
    flat_bf = hidden_in.reshape(token_count, D)
    flat_rows = flat_bf.astype(jnp.float32)
    s_query, s_key, s_value = project(flat_bf, bin_attn, student_vec, seq_here)
    t_query, t_key, t_value = project(flat_bf, teach_attn, teacher_vec, seq_here)
    key_all, value_all, t_key_all, t_value_all = (
        lax.all_gather(s_key, "ctx", axis=1, tiled=True),
        lax.all_gather(s_value, "ctx", axis=1, tiled=True),
        lax.all_gather(t_key, "ctx", axis=1, tiled=True),
        lax.all_gather(t_value, "ctx", axis=1, tiled=True),
    )

    def forward_seq(seq_item):
        return attend_forward(seq_item[0], seq_item[1], seq_item[2], query_pos, key_pos)

    t_heads = lax.map(forward_seq, (t_query, t_key_all, t_value_all))[0]
    t_parts = dense_part(
        flat_rows,
        t_heads.reshape(token_count, D).astype(jnp.bfloat16),
        teach_attn[3],
        teach_in,
        teach_out,
        teacher_vec,
    )
    target = t_parts[7]
    s_heads, s_lse = lax.map(forward_seq, (s_query, key_all, value_all))
    heads_bf = s_heads.reshape(token_count, D).astype(jnp.bfloat16)
    branch, first_norm, first_bf, inner_pre, activated, feed_out, second_sum, output = dense_part(
        flat_rows, heads_bf, bin_attn[3], bin_in, bin_out, student_vec
    )
    mismatch = output - target
    grad_output = valid_rows * mismatch / loss_scale
    second_back = jax.vjp(layer_norm, second_sum, student_vec[6], student_vec[7])[1]
    grad_second, grad_g2, grad_c2 = second_back(grad_output)
    grad_b2 = jnp.sum(grad_second, axis=0)
    feed_bf = grad_second.astype(jnp.bfloat16)
    grad_down = left_product(activated, feed_bf)
    grad_act = right_product(feed_bf, bin_out)
    grad_inner = jax.vjp(gelu_exact, inner_pre)[1](grad_act)[0]
    grad_b1 = jnp.sum(grad_inner, axis=0)
    inner_bf = grad_inner.astype(jnp.bfloat16)
    grad_in = left_product(first_bf, inner_bf)
    grad_first = grad_second + right_product(inner_bf, bin_in)
    first_back = jax.vjp(layer_norm, flat_rows + branch, student_vec[4], student_vec[5])[1]
    grad_res, grad_g1, grad_c1 = first_back(grad_first)
    grad_bo = jnp.sum(grad_res, axis=0)
    branch_bf = grad_res.astype(jnp.bfloat16)
    grad_wo = left_product(heads_bf, branch_bf)
    grad_heads = (
        right_product(branch_bf, bin_attn[3]).astype(jnp.bfloat16).reshape(seq_here, rows_here, D)
    )

    def back_seq(seq_item):
        return attend_query_back(
            seq_item[0], seq_item[1], seq_item[2], seq_item[3], seq_item[4], query_pos, key_pos
        )

    grad_query, row_deltas, key_part, value_part = lax.map(
        back_seq, (s_query, key_all, value_all, grad_heads, s_lse)
    )
    grad_key, grad_value = (
        lax.psum_scatter(
            key_part.astype(jnp.bfloat16), "ctx", scatter_dimension=1, tiled=True
        ).astype(jnp.float32),
        lax.psum_scatter(
            value_part.astype(jnp.bfloat16), "ctx", scatter_dimension=1, tiled=True
        ).astype(jnp.float32),
    )
    grad_query = grad_query.reshape(token_count, D)
    grad_key = grad_key.reshape(token_count, D)
    grad_value = grad_value.reshape(token_count, D)
    grad_bq = jnp.sum(grad_query, axis=0)
    grad_bv = jnp.sum(grad_value, axis=0)
    query_bf = grad_query.astype(jnp.bfloat16)
    key_bf = grad_key.astype(jnp.bfloat16)
    value_bf = grad_value.astype(jnp.bfloat16)
    grad_attn = jnp.stack(
        [
            left_product(flat_bf, query_bf),
            left_product(flat_bf, key_bf),
            left_product(flat_bf, value_bf),
            grad_wo,
        ]
    )
    grad_flat = (
        grad_res
        + right_product(query_bf, bin_attn[0])
        + right_product(key_bf, bin_attn[1])
        + right_product(value_bf, bin_attn[2])
    )
    red_attn, red_in, red_down = (
        lax.psum_scatter(
            grad_attn.astype(jnp.bfloat16), "shard", scatter_dimension=1, tiled=True
        ).astype(jnp.float32),
        lax.psum_scatter(
            grad_in.astype(jnp.bfloat16), "shard", scatter_dimension=0, tiled=True
        ).astype(jnp.float32),
        lax.psum_scatter(
            grad_down.astype(jnp.bfloat16), "shard", scatter_dimension=0, tiled=True
        ).astype(jnp.float32),
    )
    red_attn, red_in, red_down = (
        lax.psum(red_attn.astype(jnp.bfloat16), "ctx").astype(jnp.float32),
        lax.psum(red_in.astype(jnp.bfloat16), "ctx").astype(jnp.float32),
        lax.psum(red_down.astype(jnp.bfloat16), "ctx").astype(jnp.float32),
    )
    keep_attn = (jnp.abs(attn_latent) <= 1.0).astype(jnp.float32)
    keep_in = (jnp.abs(ffn_in_latent) <= 1.0).astype(jnp.float32)
    keep_out = (jnp.abs(ffn_out_latent) <= 1.0).astype(jnp.float32)
    vec_grad = jnp.concatenate(
        [
            jnp.stack([grad_bq, grad_bv, grad_bo, grad_b2, grad_g1, grad_c1, grad_g2, grad_c2]),
            grad_b1.reshape(-1, D),
        ],
        axis=0,
    )
    square_sums = jnp.stack(
        [
            0.5 * jnp.sum(valid_rows * mismatch * mismatch),
            jnp.sum(valid_rows * branch * branch),
            jnp.sum(valid_rows * feed_out * feed_out),
            jnp.sum(valid_rows * second_sum * second_sum),
        ]
    )
    vec_total, sum_total = lax.psum((vec_grad, square_sums), ("ctx", "shard"))
    statistics = jnp.concatenate(
        [sum_total[0:1] / loss_scale, jnp.sqrt(sum_total[1:] / loss_scale)]
    )
    return (
        output.reshape(seq_here, rows_here, D).astype(jnp.bfloat16),
        statistics,
        grad_flat.reshape(seq_here, rows_here, D),
        red_attn * keep_attn,
        red_in * keep_in,
        red_down * keep_out,
        vec_total[1:],
        vec_total[0],
    )


def solution(mesh):
    in_specs = (
        P("shard", "ctx", None),
        P(),
        P(),
        P(None, "shard", None),
        P("shard", None),
        P("shard", None),
        P(),
        P(None, "shard", None),
        P("shard", None),
        P("shard", None),
        P(),
    )
    out_specs = (
        P("shard", "ctx", None),
        P(),
        P("shard", "ctx", None),
        P(None, "shard", None),
        P("shard", None),
        P("shard", None),
        P(),
        P(),
    )
    return jax.shard_map(body, mesh=mesh, in_specs=in_specs, out_specs=out_specs, check_vma=False)
```

profile of v0, /device:TPU:0, one launch (start us, length us, event | category | flops | bytes accessed | tf_op | source)
XLA Modules:
  0.0 1617.2 jit_solution(1807778586871363878)
XLA Ops:
  9.4 92.4 %all-gather.21.cloned.1.call-done = bf16[4,768,768]{2,1,0:T(8,128)(2,1)} async-done(((bf16[4,192,768]{2,1,0:T(8,128)(2,1)}), bf16[4,768,768]{2,1,0:T(8,128)(2,1)}) %all-gather.21.cloned.1.call-update) | async-done | bytes 4718608 | tf_op jit(solution)/shard_map/all_gather | solution.py:197
  114.1 2.6 fusion.60
  116.7 151.8 %all-gather.11.cloned.1.call-done = f32[4,768,768]{2,1,0:T(8,128)} async-done(((f32[4,192,768]{2,1,0:T(8,128)}), f32[4,768,768]{2,1,0:T(8,128)}) %all-gather.11.cloned.1.call-update) | async-done | bytes 9437200 | tf_op jit(solution)/shard_map/all_gather | solution.py:189
  268.6 4.5 abs_reduce_fusion.2
  274.9 3.1 multiply_convert_fusion.5
  282.0 20.1 %all-gather.23.cloned.1.call-done = bf16[2,1024,768]{1,2,0:T(8,128)(2,1)} async-done(((bf16[2,128,768]{1,2,0:T(8,128)(2,1)}), bf16[2,1024,768]{1,2,0:T(8,128)(2,1)}) %all-gather.23.cloned.1.call-update) | async-done | bytes 3145744 | tf_op jit(solution)/shard_map/all_gather | solution.py:209
  302.1 35.2 %all-gather.25.cloned.1.call-done = bf16[2,1024,768]{1,2,0:T(8,128)(2,1)} async-done(((bf16[2,128,768]{1,2,0:T(8,128)(2,1)}), bf16[2,1024,768]{1,2,0:T(8,128)(2,1)}) %all-gather.25.cloned.1.call-update) | async-done | bytes 3145744 | tf_op jit(solution)/shard_map/all_gather | solution.py:208
  338.0 20.3 %while.40 = (s32[]{:T(128)}, bf16[2,128,768]{2,1,0:T(8,128)(2,1)}, bf16[2,1024,768]{1,2,0:T(8,128)(2,1)}, s32[128]{0:T(128)S(1)}, bf16[2,128,768]{2,1,0:T(8,128)...) while((s32[]{:T(128)}, bf16[2,128,768]{2,1,0:T(8,128)(2,1)}, ...), condition=%wide.region_22.23_spmd.clone, body=%wide.region_15.22_spmd.clone.sunk | while | flops 414383616 | bytes 42658548 | solution.py:215
  363.9 64.1 %all-gather.27.cloned.1.call-done = bf16[768,3072]{1,0:T(8,128)(2,1)} async-done(((bf16[192,3072]{1,0:T(8,128)(2,1)}), bf16[768,3072]{1,0:T(8,128)(2,1)}) %all-gather.27.cloned.1.call-update) | async-done | bytes 4718608 | tf_op jit(solution)/shard_map/all_gather | solution.py:198
  428.1 89.4 %all-gather.29.cloned.1.call-done = bf16[3072,768]{1,0:T(8,128)(2,1)} async-done(((bf16[768,768]{1,0:T(8,128)(2,1)}), bf16[3072,768]{1,0:T(8,128)(2,1)}) %all-gather.29.cloned.1.call-update) | async-done | bytes 4718608 | tf_op jit(solution)/shard_map/all_gather | solution.py:199
  517.5 13.0 fusion.146
  533.3 150.9 %all-gather.19.cloned.1.call-done = f32[3072,768]{1,0:T(8,128)} async-done(((f32[768,768]{1,0:T(8,128)}), f32[3072,768]{1,0:T(8,128)}) %all-gather.19.cloned.1.call-update) | async-done | bytes 9437200 | tf_op jit(solution)/shard_map/all_gather | solution.py:191
  684.3 4.5 abs_reduce_fusion
  689.4 161.5 %all-gather.17.cloned.1.call-done = f32[768,3072]{1,0:T(8,128)} async-done(((f32[192,3072]{1,0:T(8,128)}), f32[768,3072]{1,0:T(8,128)}) %all-gather.17.cloned.1.call-update) | async-done | bytes 9437200 | tf_op jit(solution)/shard_map/all_gather | solution.py:190
  850.8 4.5 abs_reduce_fusion.1
  855.9 28.4 %all-gather.13.cloned.1.call-done = bf16[2,1024,768]{1,2,0:T(8,128)(2,1)} async-done(((bf16[2,128,768]{1,2,0:T(8,128)(2,1)}), bf16[2,1024,768]{1,2,0:T(8,128)(2,1)}) %all-gather.13.cloned.1.call-update) | async-done | bytes 3145744 | tf_op jit(solution)/shard_map/all_gather | solution.py:207
  884.3 35.3 %all-gather.15.cloned.1.call-done = bf16[2,1024,768]{1,2,0:T(8,128)(2,1)} async-done(((bf16[2,128,768]{1,2,0:T(8,128)(2,1)}), bf16[2,1024,768]{1,2,0:T(8,128)(2,1)}) %all-gather.15.cloned.1.call-update) | async-done | bytes 3145744 | tf_op jit(solution)/shard_map/all_gather | solution.py:206
  920.4 22.6 %while.39 = (s32[]{:T(128)}, bf16[2,128,768]{2,1,0:T(8,128)(2,1)}, f32[2,12,128]{2,1,0:T(8,128)}, bf16[2,1024,768]{1,2,0:T(8,128)(2,1)}, s32[128]{0:T(128)S(1)},...) while((s32[]{:T(128)}, bf16[2,128,768]{2,1,0:T(8,128)(2,1)}, ...), condition=%wide.region_8.9_spmd.clone, body=%wide.region_1.8_spmd.clone.sunk | while | flops 414386688 | bytes 41334212 | solution.py:225
  945.6 13.0 multiply_convert_fusion.6
  958.8 3.7 fusion.126
  965.5 11.6 fusion.149
  977.2 4.3 multiply_reduce_fusion.4
  984.6 79.8 %while.41 = (s32[]{:T(128)}, f32[2,128,768]{1,2,0:T(8,128)}, bf16[2,1024,768]{2,1,0:T(8,128)(2,1)}, bf16[2,1024,768]{2,1,0:T(8,128)(2,1)}, bf16[2,1024,768]{1,2,...) while((s32[]{:T(128)}, f32[2,128,768]{1,2,0:T(8,128)}, ...), condition=%wide.region_41.42_spmd.clone, body=%wide.region_37.41_spmd.clone.sunk | while | flops 1032224256 | bytes 197981808 | solution.py:257
  984.8 3.6 dynamic-slice_bitcast_fusion.16
  1004.7 2.6 copy.129
  1007.3 2.8 constant_dynamic-update-slice_fusion.11
  1016.8 2.6 copy.128
  1019.4 2.8 constant_dynamic-update-slice_fusion.10
  1024.6 3.6 dynamic-slice_bitcast_fusion.16
  1044.5 2.6 copy.129
  1047.1 2.8 constant_dynamic-update-slice_fusion.11
  1056.7 2.6 copy.128
  1059.3 2.8 constant_dynamic-update-slice_fusion.10
  1068.5 42.3 %reduce-scatter.5.cloned.1.call-done = bf16[2,128,768]{2,1,0:T(8,128)(2,1)} async-done(((bf16[2,1024,768]{2,1,0:T(8,128)(2,1)}), bf16[2,128,768]{2,1,0:T(8,128)(2,1)}) %reduce-scatter.5.cloned.1.call-update) | async-done | bytes 393232 | tf_op jit(solution)/shard_map/reduce_scatter | solution.py:261
  1113.3 47.4 %reduce-scatter.7.cloned.1.call-done = bf16[2,128,768]{2,1,0:T(8,128)(2,1)} async-done(((bf16[2,1024,768]{2,1,0:T(8,128)(2,1)}), bf16[2,128,768]{2,1,0:T(8,128)(2,1)}) %reduce-scatter.7.cloned.1.call-update) | async-done | bytes 393232 | tf_op jit(solution)/shard_map/reduce_scatter | solution.py:264
  1162.2 3.7 pad_maximum_fusion
  1165.9 8.6 copy.68
  1175.6 5.3 convolution_convert_fusion
  1182.1 5.1 convolution_convert_fusion.1
  1189.1 157.5 %all-reduce.6.cloned.1.call-done = bf16[4,768,768]{2,0,1:T(4,128)(2,1)} async-done(((bf16[4,768,768]{2,0,1:T(4,128)(2,1)}), bf16[4,768,768]{2,0,1:T(4,128)(2,1)}) %all-reduce.6.cloned.1.call-update) | async-done | bytes 4718608
  1346.6 2.7 constant_dynamic-slice_fusion.5
  1349.3 83.7 %reduce-scatter.11.cloned.1.call-done = bf16[768,768]{1,0:T(8,128)(2,1)} async-done(((bf16[3072,768]{1,0:T(8,128)(2,1)}), bf16[768,768]{1,0:T(8,128)(2,1)}) %reduce-scatter.11.cloned.1.call-update) | async-done | bytes 1179664 | tf_op jit(solution)/shard_map/reduce_scatter | solution.py:297
  1433.1 88.0 %reduce-scatter.9.cloned.1.call-done = bf16[192,3072]{1,0:T(8,128)(2,1)} async-done(((bf16[768,3072]{1,0:T(8,128)(2,1)}), bf16[192,3072]{1,0:T(8,128)(2,1)}) %reduce-scatter.9.cloned.1.call-update) | async-done | bytes 1179664 | tf_op jit(solution)/shard_map/reduce_scatter | solution.py:294
  1525.5 2.7 convolution_add_fusion.6
  1528.2 41.8 %all-reduce.1 = (f32[4]{0:T(128)S(1)}, f32[12,768]{1,0:T(8,128)S(1)}) all-reduce(f32[4]{0:T(128)S(1)} %pad_maximum_fusion.1, f32[12,768]{1,0:T(8,128)S(1)} %concatenate.25), channel_id=1, replica_groups=mesh['ctx'=8,'shard'=4] {'ctx','shard'}, use_global_device_ids=true, to_apply=%region_31.32 | all-reduce | flops 9220 | bytes 73760 | tf_op jit(solution)/shard_map/psum | solution.py:324
  1574.1 2.7 convolution_add_fusion.4
  1576.8 23.8 %all-reduce.8.cloned.1.call-done = (bf16[4,192,768]{2,0,1:T(4,128)(2,1)}, bf16[192,3072]{1,0:T(8,128)(2,1)}, bf16[768,768]{1,0:T(8,128)(2,1)}) async-done(((bf16[4,192,768]{2,0,1:T(4,128)(2,1)}, bf16[192,3072]{1,0:T(8,128)(2,1)}, bf16[768,768]{1,0:T(8,128)(2,1)}), (bf16[4,192,768]{2,0,1:T(4,128)(2,1)}, bf16[192,3072]{1,0:T(8,128)(2,1)}, bf16[768,768]{1,0:T(8,128)(2,1)})) %all-reduce.8.cloned.1.call-update) | async-done | bytes 3538960 | tf_op jit(solution)/shard_map/psum | solution.py:302
  1600.6 3.4 convert_select_fusion.2
  (583 shorter events, 157.0 us)
Async XLA Ops:
  7.2 94.6 %copy-start.34 = (bf16[2,128,768]{2,1,0:T(8,128)(2,1)S(1)}, bf16[2,128,768]{2,1,0:T(8,128)(2,1)}, u32[]{:S(2)}) copy-start(bf16[2,128,768]{2,1,0:T(8,128)(2,1)} %param.18) | copy-start | bytes 1179652
  7.2 94.5 %all-gather.21.cloned.1.call-start = ((), (), s32[]{:S(2)}) async-start(), calls=%async_computation.9 | async-start | bytes 5898240 | tf_op jit(solution)/shard_map/all_gather | solution.py:197
  7.9 260.6 %all-gather.11.cloned.1.call-start = ((), (), s32[]{:S(2)}) async-start(), calls=%async_computation.4 | async-start | bytes 11796480 | tf_op jit(solution)/shard_map/all_gather | solution.py:189
  8.7 293.4 %all-gather.23.cloned.1.call-start = ((), (), s32[]{:S(2)}) async-start(), calls=%async_computation.10 | async-start | bytes 3538944 | tf_op jit(solution)/shard_map/all_gather | solution.py:209
  104.4 232.8 %all-gather.25.cloned.1.call-start = ((), (), s32[]{:S(2)}) async-start(), calls=%async_computation.11 | async-start | bytes 3538944 | tf_op jit(solution)/shard_map/all_gather | solution.py:208
  107.2 320.9 %all-gather.27.cloned.1.call-start = ((), (), s32[]{:S(2)}) async-start(), calls=%async_computation.12 | async-start | bytes 5898240 | tf_op jit(solution)/shard_map/all_gather | solution.py:198
  107.8 409.6 %all-gather.29.cloned.1.call-start = ((), (), s32[]{:S(2)}) async-start(), calls=%async_computation.13 | async-start | bytes 5898240 | tf_op jit(solution)/shard_map/all_gather | solution.py:199
  108.4 575.9 %all-gather.19.cloned.1.call-start = ((), (), s32[]{:S(2)}) async-start(), calls=%async_computation.8 | async-start | bytes 11796480 | tf_op jit(solution)/shard_map/all_gather | solution.py:191
  109.2 741.7 %all-gather.17.cloned.1.call-start = ((), (), s32[]{:S(2)}) async-start(), calls=%async_computation.7 | async-start | bytes 11796480 | tf_op jit(solution)/shard_map/all_gather | solution.py:190
  109.9 774.4 %all-gather.13.cloned.1.call-start = ((), (), s32[]{:S(2)}) async-start(), calls=%async_computation.5 | async-start | bytes 3538944 | tf_op jit(solution)/shard_map/all_gather | solution.py:207
  113.5 868.0 %copy-start.55 = (f32[768]{0:T(1024)}, f32[768]{0:T(1024)S(1)}, u32[]{:S(2)}) copy-start(f32[768]{0:T(1024)S(1)} %get-tuple-element.337) | copy-start | bytes 9220
  116.7 156.3 %copy-start.101 = (f32[4]{0:T(128)S(1)}, f32[4]{0:T(128)}, u32[]{:S(2)}) copy-start(f32[4]{0:T(128)} %constant.192) | copy-start | bytes 52
  281.6 638.0 %all-gather.15.cloned.1.call-start = ((), (), s32[]{:S(2)}) async-start(), calls=%async_computation.6 | async-start | bytes 3538944 | tf_op jit(solution)/shard_map/all_gather | solution.py:206
  358.3 159.1 %copy-start.85 = (f32[3072]{0:T(1024)S(1)}, f32[3072]{0:T(1024)}, u32[]{:S(2)}) copy-start(f32[3072]{0:T(1024)} %add.353) | copy-start | bytes 36868
  358.3 159.1 %copy-start.94 = (f32[768]{0:T(1024)S(1)}, f32[768]{0:T(1024)}, u32[]{:S(2)}) copy-start(f32[768]{0:T(1024)} %get-tuple-element.327) | copy-start | bytes 9220
  358.3 159.1 %copy-start.95 = (f32[768]{0:T(1024)S(1)}, f32[768]{0:T(1024)}, u32[]{:S(2)}) copy-start(f32[768]{0:T(1024)} %get-tuple-element.328) | copy-start | bytes 9220
  358.4 159.1 %copy-start.96 = (f32[768]{0:T(1024)S(1)}, f32[768]{0:T(1024)}, u32[]{:S(2)}) copy-start(f32[768]{0:T(1024)} %get-tuple-element.329) | copy-start | bytes 9220
  361.3 749.5 %reduce-scatter.5.cloned.1.call-start = ((), (), s32[]{:S(2)}) async-start(), calls=%async_computation.14 | async-start | bytes 3538944 | tf_op jit(solution)/shard_map/reduce_scatter | solution.py:261
  517.5 13.8 copy-start.97
  530.4 158.3 %copy-start.42 = (f32[256,768]{1,0:T(8,128)}, f32[256,768]{1,0:T(8,128)S(1)}, u32[]{:S(2)}) copy-start(f32[256,768]{1,0:T(8,128)S(1)} %get-tuple-element.475) | copy-start | bytes 2359300
  943.1 15.6 slice-start
  945.3 36.3 %copy-start.21 = (f32[256,768]{1,0:T(8,128)}, f32[256,768]{1,0:T(8,128)S(1)}, u32[]{:S(2)}) copy-start(f32[256,768]{1,0:T(8,128)S(1)} %get-tuple-element.409) | copy-start | bytes 2359300
  945.3 36.3 %copy-start.72 = (f32[256]{0:T(256)}, f32[256]{0:T(256)S(1)}, u32[]{:S(2)}) copy-start(f32[256]{0:T(256)S(1)} %broadcast_multiply_fusion.6) | copy-start | bytes 3076
  945.5 36.0 %copy-start.81 = (f32[256]{0:T(256)}, f32[256]{0:T(256)S(1)}, u32[]{:S(2)}) copy-start(f32[256]{0:T(256)S(1)} %fusion.85) | copy-start | bytes 3076
  945.6 13.1 slice-start.1
  945.6 13.1 slice-start.2
  945.6 13.1 copy-start.93
  945.6 13.1 copy-start.100
  962.8 14.3 slice-start.3
  965.5 11.7 copy-start.30
  965.5 11.6 copy-start.90
  965.5 11.6 slice-start.4
  965.5 11.6 slice-start.5
  984.8 10.3 copy-start.63
  1024.6 10.2 copy-start.63
  1064.4 96.3 %reduce-scatter.7.cloned.1.call-start = ((), (), s32[]{:S(2)}) async-start(), calls=%async_computation.15 | async-start | bytes 3538944 | tf_op jit(solution)/shard_map/reduce_scatter | solution.py:264
  1065.0 281.6 %all-reduce.6.cloned.1.call-start = ((), (), s32[]{:S(2)}) async-start(), calls=%async_computation.18 | async-start | bytes 9437184
  1174.5 258.6 %reduce-scatter.11.cloned.1.call-start = ((), (), s32[]{:S(2)}) async-start(), calls=%async_computation.17 | async-start | bytes 5898240 | tf_op jit(solution)/shard_map/reduce_scatter | solution.py:297
  1181.0 340.0 %reduce-scatter.9.cloned.1.call-start = ((), (), s32[]{:S(2)}) async-start(), calls=%async_computation.16 | async-start | bytes 5898240 | tf_op jit(solution)/shard_map/reduce_scatter | solution.py:294
  1187.3 413.3 %all-reduce.8.cloned.1.call-start = ((), (), s32[]{:S(2)}) async-start(), calls=%async_computation.19 | async-start | bytes 7077888 | tf_op jit(solution)/shard_map/psum | solution.py:302
  1349.3 173.4 %copy-start.99 = (f32[768]{0:T(1024)S(1)}, f32[768]{0:T(1024)}, u32[]{:S(2)}) copy-start(f32[768]{0:T(1024)} %get-tuple-element.318) | copy-start | bytes 9220
  1349.3 173.4 %copy-start.98 = (f32[768]{0:T(1024)S(1)}, f32[768]{0:T(1024)}, u32[]{:S(2)}) copy-start(f32[768]{0:T(1024)} %get-tuple-element.325) | copy-start | bytes 9220
  1349.3 173.4 %copy-start.84 = (f32[3072]{0:T(1024)S(1)}, f32[3072]{0:T(1024)}, u32[]{:S(2)}) copy-start(f32[3072]{0:T(1024)} %get-tuple-element.477) | copy-start | bytes 36868
  1349.3 173.4 %copy-start.80 = (f32[768]{0:T(1024)S(1)}, f32[768]{0:T(1024)}, u32[]{:S(2)}) copy-start(f32[768]{0:T(1024)} %get-tuple-element.323) | copy-start | bytes 9220
  1349.3 173.5 %copy-start.79 = (f32[768]{0:T(1024)S(1)}, f32[768]{0:T(1024)}, u32[]{:S(2)}) copy-start(f32[768]{0:T(1024)} %get-tuple-element.320) | copy-start | bytes 9220
  1349.3 176.0 %copy-start.37 = (bf16[2,128,768]{2,1,0:T(8,128)(2,1)S(1)}, bf16[2,128,768]{2,1,0:T(8,128)(2,1)}, u32[]{:S(2)}) copy-start(bf16[2,128,768]{2,1,0:T(8,128)(2,1)} %reduce-scatter.7.cloned.1.call-done) | copy-start | bytes 1179652
  1521.0 50.9 %copy-start.47 = (bf16[2,128,768]{2,1,0:T(8,128)(2,1)S(1)}, bf16[2,128,768]{2,1,0:T(8,128)(2,1)}, u32[]{:S(2)}) copy-start(bf16[2,128,768]{2,1,0:T(8,128)(2,1)} %reduce-scatter.5.cloned.1.call-done) | copy-start | bytes 1179652
  1572.0 28.6 %copy-start.27 = (f32[4,192,768]{2,1,0:T(8,128)S(1)}, f32[4,192,768]{2,1,0:T(8,128)}, u32[]{:S(2)}) copy-start(f32[4,192,768]{2,1,0:T(8,128)} %param.21) | copy-start | bytes 7077892
  (122 other events, 315.8 us)
Sparse Core Ops, SparseCore 0:
  9.6 92.0 all-gather.20
  103.3 165.2 all-gather.10
  271.0 30.9 all-gather.22
  304.4 32.8 all-gather.24
  338.6 89.4 all-gather.26
  429.5 87.8 all-gather.28
  519.0 165.2 all-gather.18
  685.8 164.9 all-gather.16
  853.3 30.9 all-gather.12
  886.6 32.8 all-gather.14
  1064.5 46.2 reduce-scatter.4
  1114.4 46.2 reduce-scatter.6
  1174.6 171.9 all-reduce.5
  1348.8 84.2 reduce-scatter.10
  1435.2 85.7 reduce-scatter.8
  1525.1 75.4 all-reduce.7
where the time goes:
time: 1620 us
  waiting for transfers between devices  1280 us (79%)
  matrix products  118 us (7%)
  local copies, waits for them, and re-layouts  99.5 us (6%)
  other arithmetic  60.8 us (4%)
  blocking collectives  41.8 us (3%)
  between operations  17.2 us (1%)
    unnamed x17, waiting for transfers between devices  162 us
    all_gather x1, waiting for transfers between devices, body(): lax.all_gather(ffn_in_latent, 'shard', axis=0, tiled=True)  161 us
    all_gather x1, waiting for transfers between devices, body(): lax.all_gather(attn_latent, 'shard', axis=1, tiled=True)  152 us
    all_gather x1, waiting for transfers between devices, body(): lax.all_gather(ffn_out_latent, 'shard', axis=0, tiled=True)  151 us
    all_gather x1, waiting for transfers between devices, body(): lax.all_gather(teacher_attn, 'shard', axis=1, tiled=True)  92.4 us
    all_gather x1, waiting for transfers between devices, body(): lax.all_gather(teacher_ffn_out, 'shard', axis=0, tiled=True)  89.4 us
    reduce_scatter x1, waiting for transfers between devices, body(): lax.psum_scatter(grad_in.astype(jnp.bfloat16), 'shard', scatter_dimension...  88 us
    reduce_scatter x1, waiting for transfers between devices, body(): lax.psum_scatter(grad_down.astype(jnp.bfloat16), 'shard', scatter_dimensi...  83.7 us
  transfers between devices with their start and end apart: 16, of which 16 were waited for; matrix products, arithmetic and copies ran while one was open for 6% of the time, Pallas kernels for 0%

commit v1 on v0

--- a/solution.py
+++ b/solution.py
@@ -12,6 +12,18 @@
 attn_gains = (2.0, 2.0, 1.0, 4.0)
 heads_block = 4
 masked_score = -1e30
+
+
+def doubled_up(x, axis, dim):
+    ways, here = (lax.axis_size(axis), lax.axis_index(axis))
+    grown, reach = (x, 1)
+    while reach < ways:
+        theirs = lax.ppermute(grown, axis, [(d, d ^ reach) for d in range(ways)])
+        mine_first = jnp.concatenate([grown, theirs], axis=dim)
+        theirs_first = jnp.concatenate([theirs, grown], axis=dim)
+        grown = jnp.where(here & reach == 0, mine_first, theirs_first)
+        reach = 2 * reach
+    return grown
 
 
 def layer_norm(values, gain, shift):
@@ -188,7 +200,7 @@
     full_attn, full_in, full_out = (
         lax.all_gather(attn_latent, "shard", axis=1, tiled=True),
         lax.all_gather(ffn_in_latent, "shard", axis=0, tiled=True),
-        lax.all_gather(ffn_out_latent, "shard", axis=0, tiled=True),
+        doubled_up(ffn_out_latent, "shard", 0),
     )
     bin_attn = binarize(full_attn, jnp.sum(jnp.abs(full_attn), axis=1, keepdims=True), attn_gain, D)
     bin_in = binarize(full_in, jnp.sum(jnp.abs(full_in), axis=0, keepdims=True), 1.0, D)

time: 1620 us -> 1560 us (0.963)
  waiting for transfers between devices: 1280 us -> 1230 us
  local copies, waits for them, and re-layouts: 99.5 us -> 71.8 us
    ppermute x0 -> x2, waiting for transfers between devices: none -> 481 us  [doubled_up(): theirs = lax.ppermute(grown, axis, [(d, d ^ reach) for d in range(ways)])]
    all_gather x1 -> x0, waiting for transfers between devices: 151 us -> none  [body(): lax.all_gather(ffn_out_latent, 'shard', axis=0, tiled=True)]
    all_gather x1, waiting for transfers between devices: 152 us -> 40.7 us  [body(): lax.all_gather(attn_latent, 'shard', axis=1, tiled=True)]
    all_gather x1, waiting for transfers between devices: 89.4 us -> 0.02 us  [body(): lax.all_gather(teacher_ffn_out, 'shard', axis=0, tiled=True)]
    all_gather x1, waiting for transfers between devices: 64.1 us -> 0.02 us  [body(): lax.all_gather(teacher_ffn_in, 'shard', axis=0, tiled=True)]
    all_gather x1, waiting for transfers between devices: 161 us -> 114 us  [body(): lax.all_gather(ffn_in_latent, 'shard', axis=0, tiled=True)]
    all_gather x1, waiting for transfers between devices: 35.2 us -> 0.02 us  [body(): lax.all_gather(t_key, 'ctx', axis=1, tiled=True)]
    all_gather x1, waiting for transfers between devices: 20.1 us -> 0.02 us  [body(): lax.all_gather(t_value, 'ctx', axis=1, tiled=True)]
  transfers between devices with their start and end apart: 16 -> 17, of which waited for: 16 -> 13; matrix products, arithmetic and copies ran while one was open for 6% -> 8% of each run, Pallas kernels for 0% -> 0%
where the time goes in v1:
time: 1560 us; the launch traced here: 1550 us
  waiting for transfers between devices  1230 us (79%)
  matrix products  110 us (7%)
  other arithmetic  74 us (5%)
  local copies, waits for them, and re-layouts  71.8 us (5%)
  blocking collectives  41.7 us (3%)
  between operations  17.3 us (1%)
    ppermute x2, waiting for transfers between devices, doubled_up(): theirs = lax.ppermute(grown, axis, [(d, d ^ reach) for d in range(ways)])  481 us
    unnamed x16, waiting for transfers between devices  162 us
    all_gather x1, waiting for transfers between devices, body(): lax.all_gather(ffn_in_latent, 'shard', axis=0, tiled=True)  114 us
    all_gather x1, waiting for transfers between devices, body(): lax.all_gather(teacher_attn, 'shard', axis=1, tiled=True)  92.4 us
    reduce_scatter x1, waiting for transfers between devices, body(): lax.psum_scatter(grad_down.astype(jnp.bfloat16), 'shard', scatter_dimensi...  88 us
    reduce_scatter x1, waiting for transfers between devices, body(): lax.psum_scatter(grad_in.astype(jnp.bfloat16), 'shard', scatter_dimension...  83.9 us
    reduce_scatter x1, waiting for transfers between devices, body(): lax.psum_scatter(value_part.astype(jnp.bfloat16), 'ctx', scatter_dimensio...  47.5 us
    reduce_scatter x1, waiting for transfers between devices, body(): lax.psum_scatter(key_part.astype(jnp.bfloat16), 'ctx', scatter_dimension=...  43 us
  transfers between devices with their start and end apart: 17, of which 13 were waited for; matrix products, arithmetic and copies ran while one was open for 8% of the time, Pallas kernels for 0%

profile of v1, /device:TPU:0, one launch (start us, length us, event | category | flops | bytes accessed | tf_op | source)
XLA Modules:
  0.0 1552.2 jit_solution(4376370647232091068)
XLA Ops:
  9.4 92.4 %all-gather.18.cloned.1.call-done = bf16[4,768,768]{2,1,0:T(8,128)(2,1)} async-done(((bf16[4,192,768]{2,1,0:T(8,128)(2,1)}), bf16[4,768,768]{2,1,0:T(8,128)(2,1)}) %all-gather.18.cloned.1.call-update) | async-done | bytes 4718608 | tf_op jit(solution)/shard_map/all_gather | solution.py:209
  109.9 177.4 %collective-permute-done = f32[768,768]{1,0:T(8,128)} collective-permute-done((f32[768,768]{1,0:T(8,128)S(1)}, f32[768,768]{1,0:T(8,128)}, u32[]{:S(2)}, u32[]{:S(2)}) %collective-permute-start) | collective-permute-done | bytes 2359328 | tf_op jit(solution)/shard_map/ppermute | solution.py:21
  287.3 5.1 maximum_select_fusion.1
  292.4 40.7 %all-gather.10.cloned.1.call-done = f32[4,768,768]{2,1,0:T(8,128)} async-done(((f32[4,192,768]{2,1,0:T(8,128)}), f32[4,768,768]{2,1,0:T(8,128)}) %all-gather.10.cloned.1.call-update) | async-done | bytes 9437200 | tf_op jit(solution)/shard_map/all_gather | solution.py:201
  333.1 4.5 abs_reduce_fusion.2
  339.5 3.1 multiply_convert_fusion.5
  342.6 2.2 copy-done.1
  349.1 304.0 %collective-permute-done.1 = f32[1536,768]{1,0:T(8,128)} collective-permute-done((f32[1536,768]{1,0:T(8,128)}, f32[1536,768]{1,0:T(8,128)}, u32[]{:S(2)}, u32[]{:S(2)}) %collective-permute-start.1) | collective-permute-done | bytes 4718624 | tf_op jit(solution)/shard_map/ppermute | solution.py:21
  653.1 7.2 abs_reduce_fusion
  662.1 11.8 multiply_convert_fusion.3
  676.9 16.9 %while.40 = (s32[]{:T(128)}, bf16[2,128,768]{2,1,0:T(8,128)(2,1)S(1)}, bf16[2,1024,768]{1,2,0:T(8,128)(2,1)}, s32[128]{0:T(128)S(1)}, bf16[2,128,768]{2,1,0:T(8,...) while((s32[]{:T(128)}, bf16[2,128,768]{2,1,0:T(8,128)(2,1)S(1)}, ...), condition=%wide.region_22.23_spmd.clone, body=%wide.region_15.0_spmd.clone.sunk | while | flops 414383616 | bytes 37939880 | solution.py:227
  677.4 2.2 dynamic-slice_bitcast_fusion.15
  685.9 2.2 dynamic-slice_bitcast_fusion.15
  696.0 13.0 fusion.145
  711.2 113.6 %all-gather.16.cloned.1.call-done = f32[768,3072]{1,0:T(8,128)} async-done(((f32[192,3072]{1,0:T(8,128)}), f32[768,3072]{1,0:T(8,128)}) %all-gather.16.cloned.1.call-update) | async-done | bytes 9437200 | tf_op jit(solution)/shard_map/all_gather | solution.py:202
  824.8 4.5 abs_reduce_fusion.1
  829.3 29.0 %all-gather.12.cloned.1.call-done = bf16[2,1024,768]{1,2,0:T(8,128)(2,1)} async-done(((bf16[2,128,768]{1,2,0:T(8,128)(2,1)}), bf16[2,1024,768]{1,2,0:T(8,128)(2,1)}) %all-gather.12.cloned.1.call-update) | async-done | bytes 3145744 | tf_op jit(solution)/shard_map/all_gather | solution.py:219
  858.3 35.3 %all-gather.14.cloned.1.call-done = bf16[2,1024,768]{1,2,0:T(8,128)(2,1)} async-done(((bf16[2,128,768]{1,2,0:T(8,128)(2,1)}), bf16[2,1024,768]{1,2,0:T(8,128)(2,1)}) %all-gather.14.cloned.1.call-update) | async-done | bytes 3145744 | tf_op jit(solution)/shard_map/all_gather | solution.py:218
  893.7 18.2 %while.39 = (s32[]{:T(128)}, bf16[2,128,768]{2,1,0:T(8,128)(2,1)S(1)}, f32[2,12,128]{2,1,0:T(8,128)}, bf16[2,1024,768]{1,2,0:T(8,128)(2,1)}, s32[128]{0:T(128)S(...) while((s32[]{:T(128)}, ...), condition=%wide.region_8.9_spmd.clone, body=%wide.region_1.8_spmd.clone.sunk | while | flops 414386688 | bytes 37561012 | solution.py:237
  894.4 2.2 dynamic-slice_bitcast_fusion.13
  903.3 2.2 dynamic-slice_bitcast_fusion.13
  914.3 12.7 multiply_convert_fusion.6
  928.9 2.3 fusion.121
  931.7 2.9 fusion.148
  934.6 4.3 multiply_reduce_fusion.4
  940.2 2.5 convolution_convert_fusion.4
  942.7 55.9 %while.41 = (s32[]{:T(128)}, f32[2,128,768]{1,2,0:T(8,128)}, bf16[2,1024,768]{2,1,0:T(8,128)(2,1)}, bf16[2,1024,768]{2,1,0:T(8,128)(2,1)}, bf16[2,1024,768]{1,2,...) while((s32[]{:T(128)}, f32[2,128,768]{1,2,0:T(8,128)}, ...), condition=%wide.region_41.42_spmd.clone, body=%wide.region_37.41_spmd.clone.sunk | while | flops 1032224256 | bytes 116177744 | solution.py:269
  945.2 2.2 dynamic-slice_bitcast_fusion.16
  966.3 2.7 constant_dynamic-update-slice_fusion.11
  973.0 2.2 dynamic-slice_bitcast_fusion.16
  994.1 2.6 constant_dynamic-update-slice_fusion.11
  1002.1 43.0 %reduce-scatter.5.cloned.1.call-done = bf16[2,128,768]{2,1,0:T(8,128)(2,1)} async-done(((bf16[2,1024,768]{2,1,0:T(8,128)(2,1)}), bf16[2,128,768]{2,1,0:T(8,128)(2,1)}) %reduce-scatter.5.cloned.1.call-update) | async-done | bytes 393232 | tf_op jit(solution)/shard_map/reduce_scatter | solution.py:273
  1045.0 2.5 fusion.50
  1047.6 47.5 %reduce-scatter.7.cloned.1.call-done = bf16[2,128,768]{2,1,0:T(8,128)(2,1)} async-done(((bf16[2,1024,768]{2,1,0:T(8,128)(2,1)}), bf16[2,128,768]{2,1,0:T(8,128)(2,1)}) %reduce-scatter.7.cloned.1.call-update) | async-done | bytes 393232 | tf_op jit(solution)/shard_map/reduce_scatter | solution.py:276
  1096.6 3.7 pad_maximum_fusion
  1100.3 8.5 copy.68
  1110.5 4.7 convolution_convert_fusion.1
  1116.8 3.7 convolution_convert_fusion
  1122.4 158.6 %all-reduce.6.cloned.1.call-done = bf16[4,768,768]{2,0,1:T(4,128)(2,1)} async-done(((bf16[4,768,768]{2,0,1:T(4,128)(2,1)}), bf16[4,768,768]{2,0,1:T(4,128)(2,1)}) %all-reduce.6.cloned.1.call-update) | async-done | bytes 4718608
  1281.0 2.7 constant_dynamic-slice_fusion.5
  1283.6 83.9 %reduce-scatter.9.cloned.1.call-done = bf16[192,3072]{1,0:T(8,128)(2,1)} async-done(((bf16[768,3072]{1,0:T(8,128)(2,1)}), bf16[192,3072]{1,0:T(8,128)(2,1)}) %reduce-scatter.9.cloned.1.call-update) | async-done | bytes 1179664 | tf_op jit(solution)/shard_map/reduce_scatter | solution.py:306
  1367.6 88.0 %reduce-scatter.11.cloned.1.call-done = bf16[768,768]{1,0:T(8,128)(2,1)} async-done(((bf16[3072,768]{1,0:T(8,128)(2,1)}), bf16[768,768]{1,0:T(8,128)(2,1)}) %reduce-scatter.11.cloned.1.call-update) | async-done | bytes 1179664 | tf_op jit(solution)/shard_map/reduce_scatter | solution.py:309
  1467.0 2.7 convolution_add_fusion.6
  1469.7 41.7 %all-reduce.1 = (f32[4]{0:T(128)S(1)}, f32[12,768]{1,0:T(8,128)S(1)}) all-reduce(f32[4]{0:T(128)S(1)} %pad_maximum_fusion.1, f32[12,768]{1,0:T(8,128)S(1)} %concatenate.41), channel_id=1, replica_groups=mesh['ctx'=8,'shard'=4] {'ctx','shard'}, use_global_device_ids=true, to_apply=%region_31.32 | all-reduce | flops 9220 | bytes 73760 | tf_op jit(solution)/shard_map/psum | solution.py:336
  1513.4 2.1 convolution_add_fusion.5
  1515.5 2.7 convolution_add_fusion.4
  1518.2 17.2 %all-reduce.8.cloned.1.call-done = (bf16[4,192,768]{2,0,1:T(4,128)(2,1)}, bf16[192,3072]{1,0:T(8,128)(2,1)}, bf16[768,768]{1,0:T(8,128)(2,1)}) async-done(((bf16[4,192,768]{2,0,1:T(4,128)(2,1)}, bf16[192,3072]{1,0:T(8,128)(2,1)}, bf16[768,768]{1,0:T(8,128)(2,1)}), (bf16[4,192,768]{2,0,1:T(4,128)(2,1)}, bf16[192,3072]{1,0:T(8,128)(2,1)}, bf16[768,768]{1,0:T(8,128)(2,1)})) %all-reduce.8.cloned.1.call-update) | async-done | bytes 3538960 | tf_op jit(solution)/shard_map/psum | solution.py:314
  1535.4 3.4 convert_select_fusion.2
  (407 shorter events, 130.1 us)
Async XLA Ops:
  7.2 94.6 %copy-start.12 = (bf16[2,128,768]{2,1,0:T(8,128)(2,1)S(1)}, bf16[2,128,768]{2,1,0:T(8,128)(2,1)}, u32[]{:S(2)}) copy-start(bf16[2,128,768]{2,1,0:T(8,128)(2,1)} %param.18) | copy-start | bytes 1179652
  7.2 94.5 %all-gather.18.cloned.1.call-start = ((), (), s32[]{:S(2)}) async-start(), calls=%async_computation.8 | async-start | bytes 5898240 | tf_op jit(solution)/shard_map/all_gather | solution.py:209
  7.9 325.2 %all-gather.10.cloned.1.call-start = ((), (), s32[]{:S(2)}) async-start(), calls=%async_computation.4 | async-start | bytes 11796480 | tf_op jit(solution)/shard_map/all_gather | solution.py:201
  8.7 668.2 %all-gather.20.cloned.1.call-start = ((), (), s32[]{:S(2)}) async-start(), calls=%async_computation.9 | async-start | bytes 3538944 | tf_op jit(solution)/shard_map/all_gather | solution.py:221
  104.4 572.4 %all-gather.22.cloned.1.call-start = ((), (), s32[]{:S(2)}) async-start(), calls=%async_computation.10 | async-start | bytes 3538944 | tf_op jit(solution)/shard_map/all_gather | solution.py:220
  106.2 2.9 copy-start.8
  106.3 3.0 copy-start.32
  107.2 588.8 %all-gather.24.cloned.1.call-start = ((), (), s32[]{:S(2)}) async-start(), calls=%async_computation.11 | async-start | bytes 5898240 | tf_op jit(solution)/shard_map/all_gather | solution.py:210
  107.8 588.2 %all-gather.26.cloned.1.call-start = ((), (), s32[]{:S(2)}) async-start(), calls=%async_computation.12 | async-start | bytes 5898240 | tf_op jit(solution)/shard_map/all_gather | solution.py:211
  108.4 716.5 %all-gather.16.cloned.1.call-start = ((), (), s32[]{:S(2)}) async-start(), calls=%async_computation.7 | async-start | bytes 11796480 | tf_op jit(solution)/shard_map/all_gather | solution.py:202
  109.1 749.2 %all-gather.12.cloned.1.call-start = ((), (), s32[]{:S(2)}) async-start(), calls=%async_computation.5 | async-start | bytes 3538944 | tf_op jit(solution)/shard_map/all_gather | solution.py:219
  109.2 178.1 %collective-permute-start = (f32[768,768]{1,0:T(8,128)S(1)}, f32[768,768]{1,0:T(8,128)}, u32[]{:S(2)}, u32[]{:S(2)}) collective-permute-start(f32[768,768]{1,0:T(8,128)S(1)} %copy-done.8), channel_id=1, source_target_pairs={{0,1},{1,0},{2,3},{3,2},{4,5},{5,4},{6,7},{7,6},{8,9},{9,8},{10,11... | collective-permute-start | bytes 7077896 | tf_op jit(solution)/shard_map/ppermute | solution.py:21
  292.4 45.2 %copy-start.52 = (f32[4]{0:T(128)S(1)}, f32[4]{0:T(128)}, u32[]{:S(2)}) copy-start(f32[4]{0:T(128)} %constant.194) | copy-start | bytes 52
  292.4 360.8 %collective-permute-start.1 = (f32[1536,768]{1,0:T(8,128)}, f32[1536,768]{1,0:T(8,128)}, u32[]{:S(2)}, u32[]{:S(2)}) collective-permute-start(f32[1536,768]{1,0:T(8,128)} %maximum_select_fusion.1), channel_id=1, source_target_pairs={{0,2},{1,3},{2,0},{3,1},{4,6},{5,7},{6,4},{7,5},{8,10},{9,11},{10,... | collective-permute-start | bytes 14155784 | tf_op jit(solution)/shard_map/ppermute | solution.py:21
  333.1 6.4 copy-start
  342.6 3.8 copy-start.53
  342.6 3.9 slice-start.6
  342.6 4.5 slice-start.5
  342.6 4.5 copy-start.54
  346.2 547.4 %all-gather.14.cloned.1.call-start = ((), (), s32[]{:S(2)}) async-start(), calls=%async_computation.6 | async-start | bytes 3538944 | tf_op jit(solution)/shard_map/all_gather | solution.py:218
  676.6 368.5 %reduce-scatter.5.cloned.1.call-start = ((), (), s32[]{:S(2)}) async-start(), calls=%async_computation.13 | async-start | bytes 3538944 | tf_op jit(solution)/shard_map/reduce_scatter | solution.py:273
  829.3 84.9 %copy-start.44 = (f32[3072]{0:T(1024)}, f32[3072]{0:T(1024)S(1)}, u32[]{:S(2)}) copy-start(f32[3072]{0:T(1024)S(1)} %broadcast_multiply_fusion) | copy-start | bytes 36868
  893.7 18.3 %copy-start.40 = (f32[768]{0:T(1024)S(1)}, f32[768]{0:T(1024)}, u32[]{:S(2)}) copy-start(f32[768]{0:T(1024)} %get-tuple-element.338) | copy-start | bytes 9220
  911.9 15.1 copy-start.15
  911.9 15.0 slice-start.3
  913.9 25.0 %copy-start.2 = (f32[256,768]{1,0:T(8,128)}, f32[256,768]{1,0:T(8,128)S(1)}, u32[]{:S(2)}) copy-start(f32[256,768]{1,0:T(8,128)S(1)} %get-tuple-element.411) | copy-start | bytes 2359300
  914.2 24.8 %copy-start.42 = (f32[256]{0:T(256)}, f32[256]{0:T(256)S(1)}, u32[]{:S(2)}) copy-start(f32[256]{0:T(256)S(1)} %fusion.84) | copy-start | bytes 3076
  914.2 12.7 slice-start.4
  914.2 12.7 copy-start.51
  928.9 5.6 slice-start
  931.7 2.9 copy-start.10
  931.7 2.9 copy-start.49
  931.7 2.9 slice-start.1
  934.6 4.4 copy-start.24
  939.4 3.4 copy-start.34
  964.3 4.6 copy-start.19
  992.2 4.6 copy-start.19
  998.6 96.4 %reduce-scatter.7.cloned.1.call-start = ((), (), s32[]{:S(2)}) async-start(), calls=%async_computation.14 | async-start | bytes 3538944 | tf_op jit(solution)/shard_map/reduce_scatter | solution.py:276
  999.4 281.6 %all-reduce.6.cloned.1.call-start = ((), (), s32[]{:S(2)}) async-start(), calls=%async_computation.17 | async-start | bytes 9437184
  1108.8 258.7 %reduce-scatter.9.cloned.1.call-start = ((), (), s32[]{:S(2)}) async-start(), calls=%async_computation.15 | async-start | bytes 5898240 | tf_op jit(solution)/shard_map/reduce_scatter | solution.py:306
  1115.2 340.4 %reduce-scatter.11.cloned.1.call-start = ((), (), s32[]{:S(2)}) async-start(), calls=%async_computation.16 | async-start | bytes 5898240 | tf_op jit(solution)/shard_map/reduce_scatter | solution.py:309
  1120.5 414.9 %all-reduce.8.cloned.1.call-start = ((), (), s32[]{:S(2)}) async-start(), calls=%async_computation.18 | async-start | bytes 7077888 | tf_op jit(solution)/shard_map/psum | solution.py:314
  1122.4 333.9 %copy-start.41 = (f32[768]{0:T(1024)S(1)}, f32[768]{0:T(1024)}, u32[]{:S(2)}) copy-start(f32[768]{0:T(1024)} %get-tuple-element.320) | copy-start | bytes 9220
  1283.6 179.8 %copy-start.22 = (f32[2,128,768]{1,2,0:T(8,128)S(1)}, f32[2,128,768]{1,2,0:T(8,128)}, u32[]{:S(2)}) copy-start(f32[2,128,768]{1,2,0:T(8,128)} %get-tuple-element.150) | copy-start | bytes 2359300
  1283.6 182.5 %copy-start.14 = (bf16[2,128,768]{2,1,0:T(8,128)(2,1)S(1)}, bf16[2,128,768]{2,1,0:T(8,128)(2,1)}, u32[]{:S(2)}) copy-start(bf16[2,128,768]{2,1,0:T(8,128)(2,1)} %reduce-scatter.7.cloned.1.call-done) | copy-start | bytes 1179652
  1455.5 11.5 copy-start.36
  1455.6 57.8 %copy-start.23 = (bf16[2,128,768]{2,1,0:T(8,128)(2,1)S(1)}, bf16[2,128,768]{2,1,0:T(8,128)(2,1)}, u32[]{:S(2)}) copy-start(bf16[2,128,768]{2,1,0:T(8,128)(2,1)} %reduce-scatter.5.cloned.1.call-done) | copy-start | bytes 1179652
  1513.4 22.0 %copy-start.6 = (f32[4,192,768]{2,1,0:T(8,128)S(1)}, f32[4,192,768]{2,1,0:T(8,128)}, u32[]{:S(2)}) copy-start(f32[4,192,768]{2,1,0:T(8,128)} %param.21) | copy-start | bytes 7077892
  (34 other events, 66.9 us)
Sparse Core Ops, SparseCore 0:
  9.6 92.0 all-gather.17
  103.3 229.7 all-gather.9
  335.6 33.8 all-gather.19
  371.8 32.8 all-gather.21
  406.0 127.4 all-gather.23
  535.0 122.0 all-gather.25
  658.6 166.1 all-gather.15
  827.3 30.9 all-gather.11
  860.8 32.8 all-gather.13
  998.8 46.2 reduce-scatter.4
  1048.8 46.2 reduce-scatter.6
  1109.0 171.9 all-reduce.5
  1283.3 84.2 reduce-scatter.8
  1369.7 85.7 reduce-scatter.10
  1459.6 75.7 all-reduce.7
